TPU v7x, 32 devices: a whole 2x2x4 slice. The times are simulated.
32 devices in a mesh: parts: 2 (over y), row: 4 (over x, core), col: 4 (over z).
Axes of the slice: x: 2, y: 2, z: 4, core: 2. Of those that a mesh axis runs over, the one named last changes fastest.
Arguments:
- alignment_tensor: bfloat16 [256, 256, 256], P(('parts', 'col'), 'row'), parts along dimension 0, may hold values from -6 to 6
- standardizer_scaling: float32 [256], replicated, may hold values from 0.25 to 1.75
- standardizer_offset: float32 [256], replicated, may hold values from -3 to 3
- first_projector: bfloat16 [256, 32], replicated, may hold values from -0.375 to 0.375
- second_projector: bfloat16 [256, 32], replicated, may hold values from -0.375 to 0.375
- final_projector: bfloat16 [1024, 128], replicated, may hold values from -1 to 1
- final_offset: float32 [128], replicated, may hold values from -3 to 3
- amino_strand_label: int32 [512], P('parts'), parts along dimension 0, may hold values from 0 to 7, never falling along the last dimension, each value on 1 to 128 neighbouring positions
- matched_strand_count: int32 [16, 8], P('parts'), parts along dimension 0, may hold values from 32 to 128, as said below
- couple_delta_adjoint: bfloat16 [512, 256, 128], P(('parts', 'row'), 'col'), parts along dimension 0, may hold values from -6 to 6
Outputs:
- pair_update: bfloat16 [512, 256, 128], P(('parts', 'row'), 'col'), parts along dimension 0
- adjoint_first_factor: bfloat16 [256, 8192], P(('parts', 'col'), 'row'), parts along dimension 0
- grad_right: bfloat16 [256, 8192], P(('parts', 'col'), 'row'), parts along dimension 0
- grad_w_out: float32 [2048, 128], P('parts'), parts along dimension 0
There are 2 independent parts, one for each index of `parts`. A program takes and returns all parts, laid end to end along the dimension named above; an argument that names none is the same for every part. Nothing has to cross between parts.
Inputs may be any that keep to these rules, and one draw needn't show every extreme that they name: `amino_strand_label`: chain numbers never fall along the residues; a chain has 1 to 128 residues. `matched_strand_count`: every entry is a multiple of 32.
All inputs are finite; a program needn't handle non-finite values.
Results may differ from a plain program's by a relative error of at most 0.018.
Values may be sent and summed in bfloat16 or wider, within the bound.
A program may use at most 256 MiB of HBM per device.

v0:
```python
import jax
import jax.numpy as jnp
from jax import lax
from jax.sharding import PartitionSpec as P

PROJECTED_SIZE = 32
CZ = 128
WINDOW_AMINOS = 256
DEPTH_STEP = 32
CHAINS = 8
LEVELS = 4


def standardize_entries(alignment_tensor, standard_multiplier, additive_offset):
    incoming_entries = alignment_tensor.astype(jnp.float32)
    center = incoming_entries - jnp.mean(incoming_entries, axis=-1, keepdims=True)
    spread = jnp.mean(center * center, axis=-1, keepdims=True)
    return (center * lax.rsqrt(spread + 1e-05) * standard_multiplier + additive_offset).astype(
        jnp.bfloat16
    )


def shards(
    alignment_tensor,
    standardizer_scaling,
    standardizer_offset,
    first_projector,
    second_projector,
    final_projector,
    final_offset,
    amino_strand_label,
    matched_strand_count,
    couple_delta_adjoint,
):
    homolog_portion, incoming_matrix, embedding_extent = alignment_tensor.shape
    cols = couple_delta_adjoint.shape[1]
    standardized_entries = standardize_entries(
        alignment_tensor, standardizer_scaling, standardizer_offset
    ).reshape(-1, embedding_extent)
    first_factor = (
        jnp.dot(standardized_entries, first_projector, preferred_element_type=jnp.float32)
        .astype(jnp.bfloat16)
        .reshape(homolog_portion, incoming_matrix * PROJECTED_SIZE)
    )
    second_factor = (
        jnp.dot(standardized_entries, second_projector, preferred_element_type=jnp.float32)
        .astype(jnp.bfloat16)
        .reshape(homolog_portion, incoming_matrix * PROJECTED_SIZE)
    )
    left_panel = lax.all_gather(first_factor, "col", axis=0, tiled=True)
    right_rows = lax.all_gather(second_factor, "row", axis=1, tiled=True)
    right_panel = lax.all_to_all(right_rows, "col", split_axis=1, concat_axis=0, tiled=True)
    row_start = lax.axis_index("row") * incoming_matrix
    col_start = lax.axis_index("col") * cols
    chains = jnp.arange(CHAINS, dtype=jnp.int32)
    row_hot = (
        lax.dynamic_slice_in_dim(amino_strand_label, row_start, incoming_matrix, 0)[:, None]
        == chains[None, :]
    ).astype(jnp.float32)
    col_hot = (
        lax.dynamic_slice_in_dim(amino_strand_label, col_start, cols, 0)[:, None] == chains[None, :]
    ).astype(jnp.float32)
    table = matched_strand_count.astype(jnp.float32)
    depth = jnp.dot(
        jnp.dot(row_hot, table, precision=lax.Precision.HIGHEST),
        col_hot.T,
        precision=lax.Precision.HIGHEST,
    )
    count = LEVELS

    def forward_level(level, acc):
        low = level * DEPTH_STEP
        left_level = lax.dynamic_slice_in_dim(left_panel, low, DEPTH_STEP, 0)
        right_level = lax.dynamic_slice_in_dim(right_panel, low, DEPTH_STEP, 0)
        prod = lax.dot_general(
            left_level, right_level, (((0,), (0,)), ((), ())), preferred_element_type=jnp.float32
        )
        prod = (
            prod.reshape(incoming_matrix, PROJECTED_SIZE, cols, PROJECTED_SIZE)
            .transpose(0, 2, 1, 3)
            .reshape(incoming_matrix, cols, PROJECTED_SIZE * PROJECTED_SIZE)
        )
        keep = (depth > low.astype(jnp.float32)).astype(jnp.float32)
        return acc + keep[:, :, None] * prod

    acc = lax.fori_loop(
        0,
        count,
        forward_level,
        jnp.zeros((incoming_matrix, cols, PROJECTED_SIZE * PROJECTED_SIZE), jnp.float32),
    )
    outer = (acc / depth[:, :, None]).astype(jnp.bfloat16)
    flat_outer = outer.reshape(-1, PROJECTED_SIZE * PROJECTED_SIZE)
    pair = (
        jnp.dot(flat_outer, final_projector, preferred_element_type=jnp.float32) + final_offset
    ).astype(jnp.bfloat16)
    pair_update = pair.reshape(incoming_matrix, cols, CZ)
    flat_grad = couple_delta_adjoint.reshape(-1, CZ)
    back = lax.dot_general(
        flat_grad, final_projector, (((1,), (1,)), ((), ())), preferred_element_type=jnp.float32
    )
    scaled = (
        back.reshape(incoming_matrix, cols, PROJECTED_SIZE * PROJECTED_SIZE) / depth[:, :, None]
    ).astype(jnp.bfloat16)
    turned = (
        scaled.reshape(incoming_matrix, cols, PROJECTED_SIZE, PROJECTED_SIZE)
        .transpose(0, 2, 1, 3)
        .reshape(incoming_matrix * PROJECTED_SIZE, cols * PROJECTED_SIZE)
    )

    def backward_level(level, grads):
        left_grad, right_grad = grads
        low = level * DEPTH_STEP
        left_level = lax.dynamic_slice_in_dim(left_panel, low, DEPTH_STEP, 0)
        right_level = lax.dynamic_slice_in_dim(right_panel, low, DEPTH_STEP, 0)
        keep = (depth > low.astype(jnp.float32)).astype(jnp.bfloat16)
        keep_wide = jnp.broadcast_to(
            keep[:, None, :, None], (incoming_matrix, PROJECTED_SIZE, cols, PROJECTED_SIZE)
        ).reshape(incoming_matrix * PROJECTED_SIZE, cols * PROJECTED_SIZE)
        masked = turned * keep_wide
        left_piece = lax.dot_general(
            right_level, masked, (((1,), (1,)), ((), ())), preferred_element_type=jnp.float32
        )
        right_piece = jnp.dot(left_level, masked, preferred_element_type=jnp.float32)
        left_grad = lax.dynamic_update_slice_in_dim(left_grad, left_piece, low, 0)
        right_grad = lax.dynamic_update_slice_in_dim(right_grad, right_piece, low, 0)
        return (left_grad, right_grad)

    seqs = left_panel.shape[0]
    start_grads = (
        jnp.zeros((seqs, incoming_matrix * PROJECTED_SIZE), jnp.float32),
        jnp.zeros((seqs, cols * PROJECTED_SIZE), jnp.float32),
    )
    left_grad, right_grad = lax.fori_loop(0, count, backward_level, start_grads)
    weight_part = lax.dot_general(
        flat_outer, flat_grad, (((0,), (0,)), ((), ())), preferred_element_type=jnp.float32
    )
    adjoint_first_factor = lax.psum_scatter(
        left_grad.astype(jnp.bfloat16), "col", scatter_dimension=0, tiled=True
    )
    right_parts = lax.all_to_all(
        right_grad.astype(jnp.bfloat16), "col", split_axis=0, concat_axis=1, tiled=True
    ).astype(right_grad.dtype)
    grad_right = lax.psum_scatter(
        right_parts.astype(jnp.bfloat16), "row", scatter_dimension=1, tiled=True
    )
    weight_total = lax.psum(weight_part, ("row", "col"))
    grad_w_out = weight_total / WINDOW_AMINOS
    return (pair_update, adjoint_first_factor, grad_right, grad_w_out)


def solution(mesh):
    in_specs = (
        P(("parts", "col"), "row", None),
        P(),
        P(),
        P(),
        P(),
        P(),
        P(),
        P("parts"),
        P("parts", None),
        P(("parts", "row"), "col", None),
    )
    out_specs = (
        P(("parts", "row"), "col", None),
        P(("parts", "col"), "row"),
        P(("parts", "col"), "row"),
        P("parts", None),
    )
    return jax.shard_map(shards, mesh=mesh, in_specs=in_specs, out_specs=out_specs, check_vma=False)
```

profile of v0, /device:TPU:0, one launch (start us, length us, event | category | flops | bytes accessed | tf_op | source)
XLA Modules:
  0.0 1022.6 jit_solution(9267214551704113431)
XLA Ops:
  15.4 8.6 all_gather.7
  24.8 4.9 all-to-all-start
  30.9 4.6 divide_convert_fusion
  36.7 15.6 %copy.44 = bf16[64,64,1024]{1,2,0:T(8,128)(2,1)} copy(bf16[64,64,1024]{2,1,0:T(8,128)(2,1)} %divide_convert_fusion) | data formatting | bytes 16777216 | tf_op jit(solution)/shard_map/convert_element_type | solution.py:104
  52.3 30.2 %copy.45 = bf16[64,32,64,32]{3,2,1,0:T(8,128)(2,1)} copy(bf16[64,32,64,32]{2,3,1,0:T(8,128)(2,1)} %bitcast.45) | data formatting | bytes 16777216 | tf_op jit(solution)/shard_map/transpose | solution.py:107
  82.6 43.6 %reshape.96 = bf16[2048,2048]{1,0:T(8,128)(2,1)} reshape(bf16[64,32,64,32]{3,2,1,0:T(8,128)(2,1)} %copy.45) | data formatting | bytes 16777216 | tf_op jit(solution)/shard_map/reshape | solution.py:108
  126.1 16.3 %all_gather.6 = bf16[128,2048]{1,0:T(8,128)(2,1)S(1)} all-gather(bf16[32,2048]{1,0:T(8,128)(2,1)S(1)} %reshape.91), channel_id=1, replica_groups=mesh['parts'=2,'row'=4,'col'=4] {'col'}, dimensions={0}, use_global_device_ids=true | all-gather | bytes 655360 | tf_op jit(solution)/shard_map/all_gather | solution.py:50
  142.4 510.9 %while.30 = (s32[]{:T(128)}, f32[64,64,1024]{1,2,0:T(8,128)}, f32[64,64]{1,0:T(8,128)S(1)}, bf16[128,2048]{1,0:T(8,128)(2,1)S(1)}, bf16[128,2048]{1,0:T(8,128)(2...) while((s32[]{:T(128)}, f32[64,64,1024]{1,2,0:T(8,128)}, f32[64,64]{1,0:T(8,128)S(1)}, ...), condition=%wide.region_3.0_spmd.clone, body=%wide.region_2.0_spmd.clone.sunk | while | flops 281026560 | bytes 134530192 | solution.py:86
  142.4 8.1 fusion.61
  150.5 40.6 %reshape.104 = f32[64,32,64,32]{3,2,1,0:T(8,128)} reshape(f32[2048,2048]{1,0:T(8,128)} %fusion.61) | data formatting | bytes 33554432 | tf_op jit(solution)/shard_map/while/body/eval_jaxpr/reshape | solution.py:79
  191.1 48.2 %copy.52 = f32[64,64,32,32]{1,3,2,0:T(8,128)} copy(f32[64,64,32,32]{3,1,2,0:T(8,128)} %bitcast.44) | data formatting | bytes 33554432 | tf_op jit(solution)/shard_map/while/body/eval_jaxpr/transpose | solution.py:80
  239.4 23.0 %fusion.62 = f32[64,64,1024]{1,2,0:T(8,128)} fusion(f32[64,64,32,32]{1,3,2,0:T(8,128)} %copy.52, f32[64,64,1024]{1,2,0:T(8,128)} %get-tuple-element.354, f32[64,64]{1,0:T(8,128)S(1)} %compare_convert_fusion.5, pred[]{:T(512)S(6)} %compare.3), kind=kLoop, calls=%fused_computation.12.clone.1 | loop fusion | flops 12582912 | bytes 50348032 | tf_op jit(solution)/shard_map/while/body/eval_jaxpr/add | solution.py:84
  262.4 8.1 fusion.61
  270.5 40.6 %reshape.104 = f32[64,32,64,32]{3,2,1,0:T(8,128)} reshape(f32[2048,2048]{1,0:T(8,128)} %fusion.61) | data formatting | bytes 33554432 | tf_op jit(solution)/shard_map/while/body/eval_jaxpr/reshape | solution.py:79
  311.1 48.2 %copy.52 = f32[64,64,32,32]{1,3,2,0:T(8,128)} copy(f32[64,64,32,32]{3,1,2,0:T(8,128)} %bitcast.44) | data formatting | bytes 33554432 | tf_op jit(solution)/shard_map/while/body/eval_jaxpr/transpose | solution.py:80
  359.3 33.4 %fusion.62 = f32[64,64,1024]{1,2,0:T(8,128)} fusion(f32[64,64,32,32]{1,3,2,0:T(8,128)} %copy.52, f32[64,64,1024]{1,2,0:T(8,128)} %get-tuple-element.354, f32[64,64]{1,0:T(8,128)S(1)} %compare_convert_fusion.5, pred[]{:T(512)S(6)} %compare.3), kind=kLoop, calls=%fused_computation.12.clone.1 | loop fusion | flops 12582912 | bytes 50348032 | tf_op jit(solution)/shard_map/while/body/eval_jaxpr/add | solution.py:84
  392.7 8.1 fusion.61
  400.8 40.6 %reshape.104 = f32[64,32,64,32]{3,2,1,0:T(8,128)} reshape(f32[2048,2048]{1,0:T(8,128)} %fusion.61) | data formatting | bytes 33554432 | tf_op jit(solution)/shard_map/while/body/eval_jaxpr/reshape | solution.py:79
  441.4 48.2 %copy.52 = f32[64,64,32,32]{1,3,2,0:T(8,128)} copy(f32[64,64,32,32]{3,1,2,0:T(8,128)} %bitcast.44) | data formatting | bytes 33554432 | tf_op jit(solution)/shard_map/while/body/eval_jaxpr/transpose | solution.py:80
  489.6 33.4 %fusion.62 = f32[64,64,1024]{1,2,0:T(8,128)} fusion(f32[64,64,32,32]{1,3,2,0:T(8,128)} %copy.52, f32[64,64,1024]{1,2,0:T(8,128)} %get-tuple-element.354, f32[64,64]{1,0:T(8,128)S(1)} %compare_convert_fusion.5, pred[]{:T(512)S(6)} %compare.3), kind=kLoop, calls=%fused_computation.12.clone.1 | loop fusion | flops 12582912 | bytes 50348032 | tf_op jit(solution)/shard_map/while/body/eval_jaxpr/add | solution.py:84
  523.0 8.1 fusion.61
  531.1 40.6 %reshape.104 = f32[64,32,64,32]{3,2,1,0:T(8,128)} reshape(f32[2048,2048]{1,0:T(8,128)} %fusion.61) | data formatting | bytes 33554432 | tf_op jit(solution)/shard_map/while/body/eval_jaxpr/reshape | solution.py:79
  571.7 48.2 %copy.52 = f32[64,64,32,32]{1,3,2,0:T(8,128)} copy(f32[64,64,32,32]{3,1,2,0:T(8,128)} %bitcast.44) | data formatting | bytes 33554432 | tf_op jit(solution)/shard_map/while/body/eval_jaxpr/transpose | solution.py:80
  620.0 33.4 %fusion.62 = f32[64,64,1024]{1,2,0:T(8,128)} fusion(f32[64,64,32,32]{1,3,2,0:T(8,128)} %copy.52, f32[64,64,1024]{1,2,0:T(8,128)} %get-tuple-element.354, f32[64,64]{1,0:T(8,128)S(1)} %compare_convert_fusion.5, pred[]{:T(512)S(6)} %compare.3), kind=kLoop, calls=%fused_computation.12.clone.1 | loop fusion | flops 12582912 | bytes 50348032 | tf_op jit(solution)/shard_map/while/body/eval_jaxpr/add | solution.py:84
  653.4 24.5 %copy.43 = f32[64,64,1024]{2,1,0:T(8,128)} copy(f32[64,64,1024]{1,2,0:T(8,128)} %get-tuple-element.223) | data formatting | bytes 33554432 | tf_op jit(solution)/shard_map/while | solution.py:86
  677.9 7.0 divide_convert_fusion.1
  684.9 3.2 copy-done.3
  688.1 3.2 convolution_bitcast_fusion
  692.5 272.7 %while.29 = (s32[]{:T(128)}, bf16[128,2048]{1,0:T(8,128)(2,1)S(1)}, bf16[128,2048]{1,0:T(8,128)(2,1)}, bf16[128,2048]{1,0:T(8,128)(2,1)S(1)}, f32[64,64]{1,0:T(8...) while((s32[]{:T(128)}, bf16[128,2048]{1,0:T(8,128)(2,1)S(1)}, ...), condition=%wide.region_5.0_spmd, body=%wide.region_4.0_spmd.sunk | while | flops 545267712 | bytes 126650592 | solution.py:134
  692.5 11.5 %broadcast_in_dim.37 = bf16[64,32,64,32]{3,2,1,0:T(8,128)(2,1)} broadcast(bf16[64,64]{1,0:T(8,128)(2,1)S(1)} %compare_convert_fusion.4), dimensions={0,2} | broadcast | bytes 8396800 | tf_op jit(solution)/shard_map/while/body/eval_jaxpr/broadcast_in_dim | solution.py:117
  703.9 43.7 %reshape.103 = bf16[2048,2048]{1,0:T(8,128)(2,1)} reshape(bf16[64,32,64,32]{3,2,1,0:T(8,128)(2,1)} %broadcast_in_dim.37) | data formatting | bytes 16777216 | tf_op jit(solution)/shard_map/while/body/eval_jaxpr/reshape | solution.py:119
  747.6 8.2 fusion.58
  758.2 2.5 fusion.57
  760.7 11.4 %broadcast_in_dim.37 = bf16[64,32,64,32]{3,2,1,0:T(8,128)(2,1)} broadcast(bf16[64,64]{1,0:T(8,128)(2,1)S(1)} %compare_convert_fusion.4), dimensions={0,2} | broadcast | bytes 8396800 | tf_op jit(solution)/shard_map/while/body/eval_jaxpr/broadcast_in_dim | solution.py:117
  772.2 43.6 %reshape.103 = bf16[2048,2048]{1,0:T(8,128)(2,1)} reshape(bf16[64,32,64,32]{3,2,1,0:T(8,128)(2,1)} %broadcast_in_dim.37) | data formatting | bytes 16777216 | tf_op jit(solution)/shard_map/while/body/eval_jaxpr/reshape | solution.py:119
  815.8 8.2 fusion.58
  826.4 2.5 fusion.57
  828.9 11.4 %broadcast_in_dim.37 = bf16[64,32,64,32]{3,2,1,0:T(8,128)(2,1)} broadcast(bf16[64,64]{1,0:T(8,128)(2,1)S(1)} %compare_convert_fusion.4), dimensions={0,2} | broadcast | bytes 8396800 | tf_op jit(solution)/shard_map/while/body/eval_jaxpr/broadcast_in_dim | solution.py:117
  840.4 43.6 %reshape.103 = bf16[2048,2048]{1,0:T(8,128)(2,1)} reshape(bf16[64,32,64,32]{3,2,1,0:T(8,128)(2,1)} %broadcast_in_dim.37) | data formatting | bytes 16777216 | tf_op jit(solution)/shard_map/while/body/eval_jaxpr/reshape | solution.py:119
  883.9 8.2 fusion.58
  894.5 2.5 fusion.57
  897.1 11.4 %broadcast_in_dim.37 = bf16[64,32,64,32]{3,2,1,0:T(8,128)(2,1)} broadcast(bf16[64,64]{1,0:T(8,128)(2,1)S(1)} %compare_convert_fusion.4), dimensions={0,2} | broadcast | bytes 8396800 | tf_op jit(solution)/shard_map/while/body/eval_jaxpr/broadcast_in_dim | solution.py:117
  908.5 43.6 %reshape.103 = bf16[2048,2048]{1,0:T(8,128)(2,1)} reshape(bf16[64,32,64,32]{3,2,1,0:T(8,128)(2,1)} %broadcast_in_dim.37) | data formatting | bytes 16777216 | tf_op jit(solution)/shard_map/while/body/eval_jaxpr/reshape | solution.py:119
  952.1 8.2 fusion.58
  962.7 2.5 fusion.57
  966.1 25.1 %all_to_all.38 = bf16[4,32,2048]{2,1,0:T(8,128)(2,1)S(1)} all-to-all(bf16[4,32,2048]{2,1,0:T(8,128)(2,1)} %bitcast.52), channel_id=1, replica_groups=mesh['parts'=2,'row'=4,'col'=4] {'col'}, dimensions={0} | all-to-all | bytes 1048576 | tf_op jit(solution)/shard_map/all_to_all | solution.py:141
  992.1 6.7 fusion.19
  1000.7 14.5 %reduce-scatter.5.cloned.1.call-done = bf16[32,2048]{1,0:T(8,128)(2,1)} async-done(((bf16[32,8192]{1,0:T(8,128)(2,1)}), bf16[32,2048]{1,0:T(8,128)(2,1)}) %reduce-scatter.5.cloned.1.call-update) | async-done | bytes 131088 | tf_op jit(solution)/shard_map/reduce_scatter | solution.py:144
  (74 shorter events, 25.1 us)
Async XLA Ops:
  8.0 22.9 %copy-start = (bf16[64,64,128]{2,1,0:T(8,128)(2,1)S(1)}, bf16[64,64,128]{2,1,0:T(8,128)(2,1)}, u32[]{:S(2)}) copy-start(bf16[64,64,128]{2,1,0:T(8,128)(2,1)} %param.23) | copy-start | bytes 3145732
  8.0 21.7 %copy-start.8 = (s32[256]{0:T(256)S(1)}, s32[256]{0:T(256)}, u32[]{:S(2)}) copy-start(s32[256]{0:T(256)} %param.21) | copy-start | bytes 3076
  8.0 21.8 %copy-start.11 = (s32[8,8]{1,0:T(8,128)S(1)}, s32[8,8]{1,0:T(8,128)}, u32[]{:S(2)}) copy-start(s32[8,8]{1,0:T(8,128)} %param.22) | copy-start | bytes 772
  8.0 22.9 %copy-start.9 = (bf16[1024,128]{1,0:T(8,128)(2,1)S(1)}, bf16[1024,128]{1,0:T(8,128)(2,1)}, u32[]{:S(2)}) copy-start(bf16[1024,128]{1,0:T(8,128)(2,1)} %param.19) | copy-start | bytes 786436
  24.8 117.6 %all-to-all-start = ((bf16[32,4,2048]{2,0,1:T(8,128)(2,1)}), bf16[32,4,2048]{2,0,1:T(8,128)(2,1)S(1)}, u32[]{:S(2)}, u32[]{:S(2)}) async-start(bf16[32,4,2048]{2,0,1:T(8,128)(2,1)} %bitcast.40), calls=%async_computation | async-start | bytes 1048576 | tf_op jit(solution)/shard_map/all_to_all | solution.py:52
  29.7 969.1 %all-reduce.2.cloned.1.call-start = ((), (), s32[]{:S(2)}) async-start(), calls=%async_computation.6 | async-start | bytes 1048576 | tf_op jit(solution)/shard_map/psum | solution.py:147
  30.3 0.6 copy-start.4
  30.9 4.6 copy-start.7
  82.5 59.9 %copy-start.5 = (f32[64,64]{1,0:T(8,128)S(1)}, f32[64,64]{1,0:T(8,128)}, u32[]{:S(2)}) copy-start(f32[64,64]{1,0:T(8,128)} %copy-done.4) | copy-start | bytes 49156
  684.9 3.2 copy-start.3
  691.3 309.4 %reduce-scatter.3.cloned.1.call-start = ((), (), s32[]{:S(2)}) async-start(), calls=%async_computation.4 | async-start | bytes 655360 | tf_op jit(solution)/shard_map/reduce_scatter | solution.py:138
  692.5 299.6 %copy-start.10 = (bf16[1024,128]{1,0:T(8,128)(2,1)S(1)}, bf16[1024,128]{1,0:T(8,128)(2,1)}, u32[]{:S(2)}) copy-start(bf16[1024,128]{1,0:T(8,128)(2,1)} %param.19) | copy-start | bytes 786436
  692.5 299.6 %copy-start.12 = (f32[128]{0:T(128)S(1)}, f32[128]{0:T(128)}, u32[]{:S(2)}) copy-start(f32[128]{0:T(128)} %param.20) | copy-start | bytes 1540
  747.6 8.2 copy-start.1
  747.6 10.6 %copy-start.2 = (bf16[2048,2048]{1,0:T(8,128)(2,1)S(1)}, bf16[2048,2048]{1,0:T(8,128)(2,1)}, u32[]{:S(2)}) copy-start(bf16[2048,2048]{1,0:T(8,128)(2,1)} %get-tuple-element.398) | copy-start | bytes 25165828 | tf_op jit(solution)/shard_map/while
  815.8 8.2 copy-start.1
  815.8 10.6 %copy-start.2 = (bf16[2048,2048]{1,0:T(8,128)(2,1)S(1)}, bf16[2048,2048]{1,0:T(8,128)(2,1)}, u32[]{:S(2)}) copy-start(bf16[2048,2048]{1,0:T(8,128)(2,1)} %get-tuple-element.398) | copy-start | bytes 25165828 | tf_op jit(solution)/shard_map/while
  883.9 8.2 copy-start.1
  883.9 10.6 %copy-start.2 = (bf16[2048,2048]{1,0:T(8,128)(2,1)S(1)}, bf16[2048,2048]{1,0:T(8,128)(2,1)}, u32[]{:S(2)}) copy-start(bf16[2048,2048]{1,0:T(8,128)(2,1)} %get-tuple-element.398) | copy-start | bytes 25165828 | tf_op jit(solution)/shard_map/while
  952.1 8.2 copy-start.1
  952.1 10.6 %copy-start.2 = (bf16[2048,2048]{1,0:T(8,128)(2,1)S(1)}, bf16[2048,2048]{1,0:T(8,128)(2,1)}, u32[]{:S(2)}) copy-start(bf16[2048,2048]{1,0:T(8,128)(2,1)} %get-tuple-element.398) | copy-start | bytes 25165828 | tf_op jit(solution)/shard_map/while
  965.2 0.8 copy-start.6
  966.1 49.1 %reduce-scatter.5.cloned.1.call-start = ((), (), s32[]{:S(2)}) async-start(), calls=%async_computation.5 | async-start | bytes 655360 | tf_op jit(solution)/shard_map/reduce_scatter | solution.py:144
Sparse Core Ops, SparseCore 0:
  691.4 92.0 all-reduce.1
Sparse Core Ops, SparseCore 1:
  966.1 24.5 reduce-scatter.2
  993.6 21.6 reduce-scatter.4
where the time goes:
time: 1040 us; the launch traced here: 1020 us
  local copies, waits for them, and re-layouts  708 us (68%)
  other arithmetic  137 us (13%)
  matrix products  91.5 us (9%)
  blocking collectives  50 us (5%)
  between operations  15.7 us (2%)
  waiting for transfers between devices  14.6 us (1%)
    transpose x4, local copies, waits for them, and re-layouts, forward_level(): prod = prod.reshape(incoming_matrix, PROJECTED_SIZE, cols, PROJECTED_SIZE...  193 us
    reshape x4, local copies, waits for them, and re-layouts, backward_level(): keep_wide = jnp.broadcast_to(keep[:, None, :, None], (incoming_matrix, PR...  174 us
    reshape x4, local copies, waits for them, and re-layouts, forward_level(): prod.reshape(incoming_matrix, PROJECTED_SIZE, cols, PROJECTED_SIZE)  162 us
    add x4, other arithmetic, forward_level(): return acc + keep[:, :, None] * prod  123 us
    broadcast_in_dim x4, local copies, waits for them, and re-layouts, backward_level(): jnp.broadcast_to(keep[:, None, :, None], (incoming_matrix, PROJECTED_SIZE...  45.8 us
    reshape x1, local copies, waits for them, and re-layouts, shards(): turned = scaled.reshape(incoming_matrix, cols, PROJECTED_SIZE, PROJECTED_...  43.6 us
    dot_general x4, matrix products, backward_level(): jnp.dot(left_level, masked, preferred_element_type=jnp.float32)  32.6 us
    dot_general x4, matrix products, forward_level(): lax.dot_general(left_level, right_level, (((0,), (0,)), ((), ())), prefer...  32.4 us
  transfers between devices with their start and end apart: 4, of which 1 were waited for; matrix products, arithmetic and copies ran while one was open for 36% of the time, Pallas kernels for 0%

commit v1 on v0

v1 whole, which is shorter than its diff:
```python
import functools

import jax
import jax.numpy as jnp
from jax import lax
from jax.experimental import pallas as pl
from jax.experimental.pallas import tpu as pltpu
from jax.sharding import PartitionSpec as P

PROJECTED_SIZE = 32
CZ = 128
WINDOW_AMINOS = 256
DEPTH_STEP = 32
CHAINS = 8
LEVELS = 4


def standardize_entries(alignment_tensor, standard_multiplier, additive_offset):
    incoming_entries = alignment_tensor.astype(jnp.float32)
    center = incoming_entries - jnp.mean(incoming_entries, axis=-1, keepdims=True)
    spread = jnp.mean(center * center, axis=-1, keepdims=True)
    return (center * lax.rsqrt(spread + 1e-05) * standard_multiplier + additive_offset).astype(
        jnp.bfloat16
    )


def pair_kernel(
    group, cols, seqs, levels,
    left_ref, right_ref, depth_ref, grad_ref, weight_ref, weight_t_ref, bias_ref, left_t_ref,
    tall_ref,
    pair_ref, left_grad_ref, right_grad_ref, weight_grad_ref,
    outer_ref, scaled_ref, back_ref,
):
    step = pl.program_id(0)
    width = group * cols
    size = PROJECTED_SIZE
    chunk = 4
    depth = depth_ref[0]
    inverse = 1.0 / depth
    row = lax.broadcasted_iota(jnp.int32, (group * seqs, width), 0)
    lane = lax.broadcasted_iota(jnp.int32, (group * seqs, width), 1)
    seq = (row % seqs).astype(jnp.float32)
    keep = jnp.where(
        jnp.logical_and(row // seqs == lane // cols, seq < depth), 1.0, 0.0
    ).astype(jnp.bfloat16)
    keep = jnp.concatenate([keep] * chunk, axis=1)
    grad = grad_ref[...]
    back = lax.dot_general(
        weight_ref[...], grad, (((1,), (1,)), ((), ())), preferred_element_type=jnp.float32
    )
    back_ref[...] = (back * inverse).astype(jnp.bfloat16)
    left = left_ref[0]
    left_grad = jnp.zeros((size, group * seqs), jnp.float32)
    rows_here = pl.ds(pl.multiple_of(step * size, size), size)
    for first in range(0, size, chunk):
        lanes = slice(first * width, (first + chunk) * width)
        right = right_ref[:, lanes] * keep
        prod = jnp.dot(left, right, preferred_element_type=jnp.float32)
        for e in range(chunk):
            outer_ref[(first + e) * size : (first + e + 1) * size, :] = (
                prod[:, e * width : (e + 1) * width] * inverse
            ).astype(jnp.bfloat16)
        scaled = jnp.concatenate(
            [back_ref[(first + e) * size : (first + e + 1) * size, :] for e in range(chunk)], axis=1
        )
        scaled_ref[rows_here, lanes] = scaled
        left_grad = left_grad + lax.dot_general(
            scaled, right, (((1,), (1,)), ((), ())), preferred_element_type=jnp.float32
        )
    left_grad_ref[0] = left_grad.astype(jnp.bfloat16)
    outer = outer_ref[...]
    pair = jnp.dot(weight_t_ref[...], outer, preferred_element_type=jnp.float32).T
    pair_ref[...] = (pair + bias_ref[...]).astype(jnp.bfloat16)
    weight_part = jnp.dot(outer, grad, preferred_element_type=jnp.float32)

    @pl.when(step == 0)
    def _():
        weight_grad_ref[...] = weight_part

    @pl.when(step > 0)
    def _():
        weight_grad_ref[...] += weight_part

    @pl.when(step == pl.num_programs(0) - 1)
    def _():
        span = 2
        part = lax.broadcasted_iota(jnp.int32, (DEPTH_STEP, span * width), 1) % width // cols
        for level in range(levels):
            wanted = jnp.where(tall_ref[...] > level * DEPTH_STEP, 1.0, 0.0).astype(jnp.bfloat16)
            wanted = jnp.concatenate([wanted] * span, axis=1)

            def piece(index, carry, level=level, wanted=wanted):
                lanes = pl.ds(pl.multiple_of(index * span * width, span * width), span * width)
                masked = scaled_ref[:, lanes] * wanted
                out = jnp.dot(left_t_ref[level], masked, preferred_element_type=jnp.float32)
                total = jnp.zeros((DEPTH_STEP, span * width), jnp.float32)
                for g in range(group):
                    total = jnp.where(part == g, out[g * DEPTH_STEP : (g + 1) * DEPTH_STEP], total)
                right_grad_ref[level * DEPTH_STEP : (level + 1) * DEPTH_STEP, lanes] = total
                return carry

            lax.fori_loop(0, size // span, piece, 0)


def shards(
    alignment_tensor,
    standardizer_scaling,
    standardizer_offset,
    first_projector,
    second_projector,
    final_projector,
    final_offset,
    amino_strand_label,
    matched_strand_count,
    couple_delta_adjoint,
):
    homolog_portion, rows, embedding_extent = alignment_tensor.shape
    cols = couple_delta_adjoint.shape[1]
    size = PROJECTED_SIZE
    entries = standardize_entries(
        alignment_tensor, standardizer_scaling, standardizer_offset
    ).reshape(-1, embedding_extent)
    both = jnp.dot(
        entries,
        jnp.concatenate([first_projector, second_projector], axis=1),
        preferred_element_type=jnp.float32,
    ).astype(jnp.bfloat16)
    first_factor = both[:, :size].reshape(homolog_portion, rows * size)
    second_factor = both[:, size:].reshape(homolog_portion, rows * size)
    left_panel = lax.all_gather(first_factor, "col", axis=0, tiled=True)
    right_rows = lax.all_gather(second_factor, "row", axis=1, tiled=True)
    right_panel = lax.all_to_all(right_rows, "col", split_axis=1, concat_axis=0, tiled=True)
    seqs = left_panel.shape[0]
    levels = seqs // DEPTH_STEP
    row_start = lax.axis_index("row") * rows
    col_start = lax.axis_index("col") * cols
    chains = jnp.arange(CHAINS, dtype=jnp.int32)
    row_hot = (
        lax.dynamic_slice_in_dim(amino_strand_label, row_start, rows, 0)[:, None] == chains[None, :]
    ).astype(jnp.float32)
    col_hot = (
        lax.dynamic_slice_in_dim(amino_strand_label, col_start, cols, 0)[:, None] == chains[None, :]
    ).astype(jnp.float32)
    table = matched_strand_count.astype(jnp.float32)
    depth = jnp.dot(
        jnp.dot(row_hot, table, precision=lax.Precision.HIGHEST),
        col_hot.T,
        precision=lax.Precision.HIGHEST,
    )
    group = max(1, 128 // cols)
    width = group * cols
    steps = rows // group
    left4 = left_panel.reshape(seqs, steps, group, size)
    left_groups = left4.transpose(1, 3, 2, 0).reshape(steps, size, group * seqs)
    left_levels = (
        left_panel.reshape(levels, DEPTH_STEP, steps, group, size)
        .transpose(0, 3, 1, 2, 4)
        .reshape(levels, group * DEPTH_STEP, steps * size)
    )
    right_turned = right_panel.reshape(seqs, cols, size).transpose(0, 2, 1)
    right_wide = jnp.broadcast_to(
        right_turned[None, :, :, None, :], (group, seqs, size, group, cols)
    ).reshape(group * seqs, size * width)
    depth_rows = depth.reshape(steps, 1, width)
    depth_tall = jnp.broadcast_to(depth_rows, (steps, size, width)).reshape(steps * size, width)
    weight = final_projector.reshape(size, size, CZ).transpose(1, 0, 2).reshape(size * size, CZ)
    flat_grad = couple_delta_adjoint.reshape(-1, CZ)
    whole = lambda shape: pl.BlockSpec(shape, lambda g: (0,) * len(shape))
    pair, left_grad, right_grad, weight_part = pl.pallas_call(
        functools.partial(pair_kernel, group, cols, seqs, levels),
        grid=(steps,),
        in_specs=[
            pl.BlockSpec((1, size, group * seqs), lambda g: (g, 0, 0)),
            whole((group * seqs, size * width)),
            pl.BlockSpec((1, 1, width), lambda g: (g, 0, 0)),
            pl.BlockSpec((width, CZ), lambda g: (g, 0)),
            whole((size * size, CZ)),
            whole((CZ, size * size)),
            whole((1, CZ)),
            whole((levels, group * DEPTH_STEP, steps * size)),
            whole((steps * size, width)),
        ],
        out_specs=[
            pl.BlockSpec((width, CZ), lambda g: (g, 0)),
            pl.BlockSpec((1, size, group * seqs), lambda g: (g, 0, 0)),
            whole((seqs, size * width)),
            whole((size * size, CZ)),
        ],
        out_shape=[
            jax.ShapeDtypeStruct((steps * width, CZ), jnp.bfloat16),
            jax.ShapeDtypeStruct((steps, size, group * seqs), jnp.bfloat16),
            jax.ShapeDtypeStruct((seqs, size * width), jnp.float32),
            jax.ShapeDtypeStruct((size * size, CZ), jnp.float32),
        ],
        scratch_shapes=[
            pltpu.VMEM((size * size, width), jnp.bfloat16),
            pltpu.VMEM((steps * size, size * width), jnp.bfloat16),
            pltpu.VMEM((size * size, width), jnp.bfloat16),
        ],
        compiler_params=pltpu.CompilerParams(
            dimension_semantics=("arbitrary",), vmem_limit_bytes=56 * 1024 * 1024
        ),
    )(
        left_groups,
        right_wide,
        depth_rows,
        flat_grad,
        weight,
        weight.T,
        final_offset[None, :],
        left_levels,
        depth_tall,
    )
    pair_update = pair.reshape(rows, cols, CZ)
    left_sum = (
        left_grad.reshape(steps, size, group, seqs).transpose(3, 0, 2, 1).reshape(seqs, rows * size)
    )
    right_sum = (
        right_grad.reshape(seqs, size, group, cols)
        .sum(axis=2)
        .astype(jnp.bfloat16)
        .transpose(0, 2, 1)
        .reshape(seqs, cols * size)
    )
    adjoint_first_factor = lax.psum_scatter(left_sum, "col", scatter_dimension=0, tiled=True)
    right_parts = lax.all_to_all(right_sum, "col", split_axis=0, concat_axis=1, tiled=True)
    grad_right = lax.psum_scatter(right_parts, "row", scatter_dimension=1, tiled=True)
    weight_total = lax.psum(weight_part, ("row", "col"))
    grad_w_out = (
        weight_total.reshape(size, size, CZ).transpose(1, 0, 2).reshape(size * size, CZ)
        / WINDOW_AMINOS
    )
    return (pair_update, adjoint_first_factor, grad_right, grad_w_out)


def solution(mesh):
    in_specs = (
        P(("parts", "col"), "row", None),
        P(),
        P(),
        P(),
        P(),
        P(),
        P(),
        P("parts"),
        P("parts", None),
        P(("parts", "row"), "col", None),
    )
    out_specs = (
        P(("parts", "row"), "col", None),
        P(("parts", "col"), "row"),
        P(("parts", "col"), "row"),
        P("parts", None),
    )
    return jax.shard_map(shards, mesh=mesh, in_specs=in_specs, out_specs=out_specs, check_vma=False)
```

time: 1040 us -> 254 us (0.24); the launches traced: 1020 us -> 253 us
  local copies, waits for them, and re-layouts: 708 us -> 36.6 us
  other arithmetic: 137 us -> 5.52 us
  matrix products: 91.5 us -> 0.9 us
  Pallas kernels: 0 us -> 63.5 us
  waiting for transfers between devices: 14.6 us -> 69.6 us
    reshape x11 -> x10, local copies, waits for them, and re-layouts: 382 us -> 16.1 us  [the longest x1 4.23 us: shards(): left_levels = left_panel.reshape(levels, DEPTH_STEP, steps, group, size)....]
    transpose x5 -> x3, local copies, waits for them, and re-layouts: 223 us -> 4.42 us  [the longest x1 2.6 us: shards(): right_turned = right_panel.reshape(seqs, cols, size).transpose(0, 2, 1)]
    add x4 -> x0, other arithmetic: 123 us -> none  [forward_level(): return acc + keep[:, :, None] * prod]
    dot_general x17 -> x1, matrix products: 91 us -> 0.44 us  [shards(): jnp.dot(entries, jnp.concatenate([first_projector, second_projector], axi...]
    psum x1, waiting for transfers between devices: 0.01 us -> 69.6 us  [shards(): weight_total = lax.psum(weight_part, ('row', 'col'))]
    pallas_call x0 -> x1, Pallas kernels: none -> 63.5 us  [shards(): pl.pallas_call(functools.partial(pair_kernel, group, cols, seqs, levels),...]
    broadcast_in_dim x4 -> x3, local copies, waits for them, and re-layouts: 45.8 us -> 2.91 us  [the longest x1 2.02 us: shards(): jnp.broadcast_to(right_turned[None, :, :, None, :], (group, seqs, size, g...]
    while x17 -> x0, local copies, waits for them, and re-layouts: 34.3 us -> none  [the longest x1 24.5 us: shards(): lax.fori_loop(0, count, forward_level, jnp.zeros((incoming_matrix, cols,...]
  transfers between devices with their start and end apart: 4 -> 4, of which waited for: 1 -> 1; matrix products, arithmetic and copies ran while one was open for 36% -> 10% of each run, Pallas kernels for 0% -> 0%
where the time goes in v1:
time: 254 us; the launch traced here: 253 us
  waiting for transfers between devices  69.6 us (27%)
  Pallas kernels  63.5 us (25%)
  blocking collectives  56.1 us (22%)
  local copies, waits for them, and re-layouts  36.6 us (14%)
  between operations  15.8 us (6%)
  other arithmetic  5.52 us (2%)
  starting transfers between devices  5.18 us (2%)
    psum x1, waiting for transfers between devices, shards(): weight_total = lax.psum(weight_part, ('row', 'col'))  69.6 us
    pallas_call x1, Pallas kernels, shards(): pl.pallas_call(functools.partial(pair_kernel, group, cols, seqs, levels),...  63.5 us
    all_to_all x1, blocking collectives, shards(): lax.all_to_all(right_sum, 'col', split_axis=0, concat_axis=1, tiled=True)  24.7 us
    all_gather x1, blocking collectives, shards(): left_panel = lax.all_gather(first_factor, 'col', axis=0, tiled=True)  22.7 us
    all_gather x1, blocking collectives, shards(): right_rows = lax.all_gather(second_factor, 'row', axis=1, tiled=True)  8.65 us
  transfers between devices with their start and end apart: 4, of which 1 were waited for; matrix products, arithmetic and copies ran while one was open for 10% of the time, Pallas kernels for 0%

profile of v1, /device:TPU:0, one launch (start us, length us, event | category | flops | bytes accessed | tf_op | source)
XLA Modules:
  0.0 253.2 jit_solution(17893046537681546317)
XLA Ops:
  8.0 0.0 copy-start
  8.1 1.6 convert_reduce_fusion
  9.7 1.9 fusion.2
  11.6 0.7 fusion.5
  12.4 0.4 convolution_convert_fusion
  12.9 0.3 copy.49
  13.2 0.5 reshape.99
  13.7 8.6 %all_gather.7 = bf16[32,8192]{1,0:T(8,128)(2,1)S(1)} all-gather(bf16[32,2048]{1,0:T(8,128)(2,1)S(1)} %reshape.99), channel_id=1, replica_groups=mesh['parts'=2,'row'=4,'col'=4] {'row'}, dimensions={1}, use_global_device_ids=true | all-gather | bytes 655360 | tf_op jit(solution)/shard_map/all_gather | solution.py:131
  22.4 0.8 copy.75
  23.2 4.9 %all-to-all-start = ((bf16[32,4,2048]{2,0,1:T(8,128)(2,1)}), bf16[32,4,2048]{2,0,1:T(8,128)(2,1)S(1)}, u32[]{:S(2)}, u32[]{:S(2)}) async-start(bf16[32,4,2048]{2,0,1:T(8,128)(2,1)} %bitcast.54), calls=%async_computation | async-start | bytes 1048576 | tf_op jit(solution)/shard_map/all_to_all | solution.py:132
  28.1 0.1 fusion.16
  28.1 0.2 fusion.9
  28.3 0.3 fusion.10
  28.6 0.1 broadcast_in_dim.10
  28.7 0.7 reshape.102.depth_ref
  29.4 0.3 copy.46
  29.7 0.5 reshape.96
  30.2 22.7 %all_gather.6 = bf16[128,2048]{1,0:T(8,128)(2,1)S(1)} all-gather(bf16[32,2048]{1,0:T(8,128)(2,1)S(1)} %reshape.96), channel_id=1, replica_groups=mesh['parts'=2,'row'=4,'col'=4] {'col'}, dimensions={0}, use_global_device_ids=true | all-gather | bytes 655360 | tf_op jit(solution)/shard_map/all_gather | solution.py:130
  52.9 1.0 copy.47
  53.9 1.6 reshape.106
  55.6 0.1 copy.52
  55.7 0.9 copy.53
  56.6 1.9 copy.74
  58.5 1.7 copy.54
  60.2 4.2 %reshape.107.left_t_ref = bf16[4,64,1024]{2,1,0:T(8,128)(2,1)} reshape(bf16[4,2,32,32,32]{4,3,2,1,0:T(8,128)(2,1)} %copy.54) | data formatting | bytes 1048576 | tf_op jit(solution)/shard_map/reshape | solution.py:158
  64.5 1.6 reshape.100
  66.1 2.6 %copy.51 = bf16[128,32,64]{0,2,1:T(8,128)(2,1)S(1)} copy(bf16[128,32,64]{1,2,0:T(8,128)(2,1)S(1)} %bitcast.55) | data formatting | bytes 1048576 | tf_op jit(solution)/shard_map/transpose | solution.py:160
  68.7 2.0 broadcast_in_dim.8
  70.7 0.3 copy.73
  71.0 3.0 %copy.55.right_ref = bf16[256,4096]{1,0:T(8,128)(2,1)} copy(bf16[256,4096]{0,1:T(8,128)(2,1)S(1)} %bitcast.59) | data formatting | bytes 4194304 | tf_op jit(solution)/shard_map/reshape | solution.py:163
  74.0 0.8 broadcast_in_dim.11
  74.8 63.5 %shard_map.129 = (bf16[4096,128]{1,0:T(8,128)(2,1)}, bf16[32,32,256]{2,1,0:T(8,128)(2,1)}, f32[128,4096]{1,0:T(8,128)}, f32[1024,128]{1,0:T(8,128)}) custom-call(bf16[32,32,256]{2,1,0:T(8,128)(2,1)} %bitcast.71, bf16[256,4096]{1,0:T(8,128)(2,1)} %copy.55.right_ref, f32[32,1,128]{2,1,0:T(1,128)} %reshape.102.depth_ref, bf16[4096,128]{1,0:T(8,128)(2,1)} %bitcast.73, ...), custom_call_target="tpu_custom_call" | custom-call | tf_op jit(solution)/shard_map/pallas_call | solution.py:169
  138.3 0.0 all-reduce.2.cloned.1.call-update
  138.3 0.0 reduce-scatter.7.cloned.1.call-start
  138.4 1.1 copy_bitcast_fusion.2
  139.5 1.0 copy.62
  140.5 0.0 reduce-scatter.7.cloned.1.call-update
  140.6 0.3 reduce-scatter.5.cloned.1.call-start
  140.8 1.9 copy.57
  142.8 0.2 reduce_sum.29
  143.0 3.2 %copy.58 = bf16[128,64,32]{2,1,0:T(8,128)(2,1)S(1)} copy(bf16[128,64,32]{0,1,2:T(8,128)(2,1)S(1)} %bitcast.67) | data formatting | bytes 1048576 | tf_op jit(solution)/shard_map/convert_element_type | solution.py:221
  146.2 2.3 all_to_all.29
  148.4 24.7 %all_to_all.35 = bf16[4,32,2048]{2,1,0:T(8,128)(2,1)S(1)} all-to-all(bf16[4,32,2048]{2,1,0:T(8,128)(2,1)S(1)} %all_to_all.29), channel_id=1, replica_groups=mesh['parts'=2,'row'=4,'col'=4] {'col'}, dimensions={0} | all-to-all | bytes 1048576 | tf_op jit(solution)/shard_map/all_to_all | solution.py:226
  173.2 0.8 copy.67
  174.0 0.0 reduce-scatter.5.cloned.1.call-update
  174.0 69.6 %all-reduce.2.cloned.1.call-done = f32[1024,128]{1,0:T(8,128)} async-done(((f32[1024,128]{1,0:T(8,128)}), f32[1024,128]{1,0:T(8,128)}) %all-reduce.2.cloned.1.call-update) | async-done | bytes 524304 | tf_op jit(solution)/shard_map/psum | solution.py:228
  243.6 1.1 broadcast_multiply_fusion
  244.7 1.1 copy.60
  (24 shorter events, 0.1 us)
Async XLA Ops:
  8.0 3.6 %copy-start = (bf16[32,64,256]{2,1,0:T(8,128)(2,1)S(1)}, bf16[32,64,256]{2,1,0:T(8,128)(2,1)}, u32[]{:S(2)}) copy-start(bf16[32,64,256]{2,1,0:T(8,128)(2,1)} %param.10) | copy-start | bytes 3145732
  8.0 3.6 %copy-start.5 = (f32[256]{0:T(256)S(1)}, f32[256]{0:T(256)}, u32[]{:S(2)}) copy-start(f32[256]{0:T(256)} %param.12) | copy-start | bytes 3076
  8.0 3.6 %copy-start.6 = (f32[256]{0:T(256)S(1)}, f32[256]{0:T(256)}, u32[]{:S(2)}) copy-start(f32[256]{0:T(256)} %param.11) | copy-start | bytes 3076
  8.0 4.3 %copy-start.3 = (bf16[256,32]{0,1:T(8,128)(2,1)S(1)}, bf16[256,32]{0,1:T(8,128)(2,1)}, u32[]{:S(2)}) copy-start(bf16[256,32]{0,1:T(8,128)(2,1)} %param.14) | copy-start | bytes 49156
  8.0 4.3 %copy-start.4 = (bf16[256,32]{0,1:T(8,128)(2,1)S(1)}, bf16[256,32]{0,1:T(8,128)(2,1)}, u32[]{:S(2)}) copy-start(bf16[256,32]{0,1:T(8,128)(2,1)} %param.13) | copy-start | bytes 49156
  12.9 15.2 %copy-start.7 = (s32[256]{0:T(256)S(1)}, s32[256]{0:T(256)}, u32[]{:S(2)}) copy-start(s32[256]{0:T(256)} %param.17) | copy-start | bytes 3076
  12.9 15.3 %copy-start.8 = (s32[8,8]{1,0:T(8,128)S(1)}, s32[8,8]{1,0:T(8,128)}, u32[]{:S(2)}) copy-start(s32[8,8]{1,0:T(8,128)} %param.18) | copy-start | bytes 772
  23.2 41.3 %all-to-all-start = ((bf16[32,4,2048]{2,0,1:T(8,128)(2,1)}), bf16[32,4,2048]{2,0,1:T(8,128)(2,1)S(1)}, u32[]{:S(2)}, u32[]{:S(2)}) async-start(bf16[32,4,2048]{2,0,1:T(8,128)(2,1)} %bitcast.54), calls=%async_computation | async-start | bytes 1048576 | tf_op jit(solution)/shard_map/all_to_all | solution.py:132
  28.1 215.5 %all-reduce.2.cloned.1.call-start = ((), (), s32[]{:S(2)}) async-start(), calls=%async_computation.5 | async-start | bytes 1048576 | tf_op jit(solution)/shard_map/psum | solution.py:228
  30.2 25.4 %copy-start.2 = (bf16[1024,128]{1,0:T(8,128)(2,1)S(1)}, bf16[1024,128]{1,0:T(8,128)(2,1)}, u32[]{:S(2)}) copy-start(bf16[1024,128]{1,0:T(8,128)(2,1)} %param.15) | copy-start | bytes 786436
  55.7 4.5 %copy-start.1 = (bf16[32,32,128]{2,1,0:T(8,128)(2,1)}, bf16[32,32,128]{2,1,0:T(8,128)(2,1)S(1)}, u32[]{:S(2)}) copy-start(bf16[32,32,128]{2,1,0:T(8,128)(2,1)S(1)} %copy.52) | copy-start | bytes 786436
  138.3 107.4 %reduce-scatter.7.cloned.1.call-start = ((), (), s32[]{:S(2)}) async-start(), calls=%async_computation.6 | async-start | bytes 655360
  140.6 105.2 %reduce-scatter.5.cloned.1.call-start = ((), (), s32[]{:S(2)}) async-start(), calls=%async_computation.4 | async-start | bytes 655360 | tf_op jit(solution)/shard_map/reduce_scatter | solution.py:227
Sparse Core Ops, SparseCore 0:
  138.5 105.0 all-reduce.1
Sparse Core Ops, SparseCore 1:
  141.7 28.7 reduce-scatter.6
  174.1 21.1 reduce-scatter.4

commit v2 on v1

--- a/solution.py
+++ b/solution.py
@@ -100,6 +100,157 @@
                 return carry
 
             lax.fori_loop(0, size // span, piece, 0)
+
+
+def to(source, target, send, recv, row, col):
+    return pltpu.make_async_remote_copy(
+        src_ref=source,
+        dst_ref=target,
+        send_sem=send,
+        recv_sem=recv,
+        device_id={"row": row, "col": col},
+        device_id_type=pl.DeviceIdType.MESH,
+    )
+
+
+def arrived(ref, sem):
+    pltpu.make_async_copy(ref, ref, sem).wait()
+
+
+def greet(n_row, n_col, me):
+    peers = n_row * n_col
+    barrier = pltpu.get_barrier_semaphore()
+
+    def signal(off, carry):
+        peer = (me + off) % peers
+        pl.semaphore_signal(
+            barrier,
+            inc=1,
+            device_id={"row": peer // n_col, "col": peer % n_col},
+            device_id_type=pl.DeviceIdType.MESH,
+        )
+        return carry
+
+    lax.fori_loop(1, peers, signal, 0)
+    pl.semaphore_wait(barrier, peers - 1)
+
+
+def sum_kernel(
+    n_row, n_col, ratio,
+    left_ref, right_ref, weight_ref,
+    left_out, right_out, weight_out,
+    left_in, right_in, weight_in, reduced, total,
+    left_send, left_recv, right_send, right_recv,
+    weight_send, weight_recv, total_send, total_recv,
+):
+    row, col = lax.axis_index("row"), lax.axis_index("col")
+    me = row * n_col + col
+    peers = n_row * n_col
+    part = weight_ref.shape[0] // peers
+    greet(n_row, n_col, me)
+
+    def weight_copy(off):
+        peer = (me + off) % peers
+        source = weight_ref.at[pl.ds(pl.multiple_of(peer * part, part), part)]
+        return to(
+            source, weight_in.at[me], weight_send.at[off], weight_recv.at[me],
+            peer // n_col, peer % n_col,
+        )
+
+    def total_copy(off):
+        peer = (me + off) % peers
+        return to(
+            reduced, total.at[me], total_send.at[off], total_recv.at[me],
+            peer // n_col, peer % n_col,
+        )
+
+    def left_copy(off):
+        peer = (col + off) % n_col
+        return to(
+            left_ref.at[peer], left_in.at[col], left_send.at[off], left_recv.at[col], row, peer
+        )
+
+    owner = col // ratio
+    slot = row * ratio + col % ratio
+
+    def right_copy(off):
+        peer = (col + off) % n_col
+        return to(
+            right_ref.at[peer], right_in.at[slot], right_send.at[off], right_recv.at[slot],
+            owner, peer,
+        )
+
+    def start(make):
+        def body(off, carry):
+            make(off).start()
+            return carry
+
+        return body
+
+    def sent(make):
+        def body(off, carry):
+            make(off).wait_send()
+            return carry
+
+        return body
+
+    lax.fori_loop(1, peers, start(weight_copy), 0)
+    lax.fori_loop(1, n_col, start(right_copy), 0)
+
+    @pl.when(owner == row)
+    def _():
+        pltpu.make_async_copy(right_ref.at[col], right_in.at[slot], right_recv.at[slot]).start()
+
+    @pl.when(owner != row)
+    def _():
+        right_copy(0).start()
+
+    lax.fori_loop(1, n_col, start(left_copy), 0)
+
+    def add_weight(off, acc):
+        peer = (me + off) % peers
+        arrived(weight_in.at[peer], weight_recv.at[peer])
+        return acc + weight_in[peer]
+
+    own = weight_ref[pl.ds(pl.multiple_of(me * part, part), part), :]
+    mine = lax.fori_loop(1, peers, add_weight, own)
+    reduced[...] = mine
+    total[me] = mine
+    lax.fori_loop(1, peers, sent(weight_copy), 0)
+    lax.fori_loop(1, peers, start(total_copy), 0)
+
+    def wait_left(off, carry):
+        peer = (col + off) % n_col
+        arrived(left_in.at[peer], left_recv.at[peer])
+        return carry
+
+    lax.fori_loop(1, n_col, wait_left, 0)
+    left_total = left_ref[col].astype(jnp.float32)
+    for off in range(1, n_col):
+        left_total = left_total + left_in[(col + off) % n_col].astype(jnp.float32)
+    left_out[...] = left_total.astype(jnp.bfloat16)
+    width = right_in.shape[2]
+    for t in range(ratio):
+        right_total = jnp.zeros(right_in.shape[1:], jnp.float32)
+        for r in range(n_row):
+            arrived(right_in.at[r * ratio + t], right_recv.at[r * ratio + t])
+            right_total = right_total + right_in[r * ratio + t].astype(jnp.float32)
+        right_out[:, t * width : (t + 1) * width] = right_total.astype(jnp.bfloat16)
+
+    def wait_total(off, carry):
+        peer = (me + off) % peers
+        arrived(total.at[peer], total_recv.at[peer])
+        return carry
+
+    lax.fori_loop(1, peers, wait_total, 0)
+    weight_out[...] = total[...].reshape(weight_out.shape)
+    lax.fori_loop(1, peers, sent(total_copy), 0)
+    lax.fori_loop(1, n_col, sent(left_copy), 0)
+    lax.fori_loop(1, n_col, sent(right_copy), 0)
+
+    @pl.when(owner != row)
+    def _():
+        right_copy(0).wait_send()
 
 
 def shards(
@@ -222,10 +373,43 @@
         .transpose(0, 2, 1)
         .reshape(seqs, cols * size)
     )
-    adjoint_first_factor = lax.psum_scatter(left_sum, "col", scatter_dimension=0, tiled=True)
-    right_parts = lax.all_to_all(right_sum, "col", split_axis=0, concat_axis=1, tiled=True)
-    grad_right = lax.psum_scatter(right_parts, "row", scatter_dimension=1, tiled=True)
-    weight_total = lax.psum(weight_part, ("row", "col"))
+    n_row, n_col = lax.axis_size("row"), lax.axis_size("col")
+    ratio = rows // cols
+    peers = n_row * n_col
+    vmem = pl.BlockSpec(memory_space=pltpu.VMEM)
+    share = seqs // n_col
+    part = weight_part.shape[0] // peers
+    dma = pltpu.SemaphoreType.DMA
+    adjoint_first_factor, grad_right, weight_total = pl.pallas_call(
+        functools.partial(sum_kernel, n_row, n_col, ratio),
+        in_specs=[vmem] * 3,
+        out_specs=[vmem] * 3,
+        out_shape=[
+            jax.ShapeDtypeStruct((share, rows * size), jnp.bfloat16),
+            jax.ShapeDtypeStruct((share, rows * size), jnp.bfloat16),
+            jax.ShapeDtypeStruct(weight_part.shape, jnp.float32),
+        ],
+        scratch_shapes=[
+            pltpu.VMEM((n_col, share, rows * size), jnp.bfloat16),
+            pltpu.VMEM((n_row * ratio, share, cols * size), jnp.bfloat16),
+            pltpu.VMEM((peers, part, CZ), jnp.float32),
+            pltpu.VMEM((part, CZ), jnp.float32),
+            pltpu.VMEM((peers, part, CZ), jnp.float32),
+            dma((n_col,)),
+            dma((n_col,)),
+            dma((n_col,)),
+            dma((n_row * ratio,)),
+            dma((peers,)),
+            dma((peers,)),
+            dma((peers,)),
+            dma((peers,)),
+        ],
+        compiler_params=pltpu.CompilerParams(collective_id=0, has_side_effects=True),
+    )(
+        left_sum.reshape(n_col, share, rows * size),
+        right_sum.reshape(n_col, share, cols * size),
+        weight_part,
+    )
     grad_w_out = (
         weight_total.reshape(size, size, CZ).transpose(1, 0, 2).reshape(size * size, CZ)
         / WINDOW_AMINOS

time: 254 us -> 203 us (0.80)
  waiting for transfers between devices: 69.6 us -> 0.01 us
  Pallas kernels: 63.5 us -> 117 us
  blocking collectives: 56.1 us -> 31.4 us
  between operations: 15.8 us -> 0.96 us
  local copies, waits for them, and re-layouts: 36.6 us -> 41.8 us
    psum x1 -> x0, waiting for transfers between devices: 69.6 us -> none  [shards(): weight_total = lax.psum(weight_part, ('row', 'col'))]
    pallas_call x0 -> x1, Pallas kernels: none -> 53.2 us  [shards(): pl.pallas_call(functools.partial(sum_kernel, n_row, n_col, ratio), in_spe...]
    all_to_all x1 -> x0, blocking collectives: 24.7 us -> none  [shards(): lax.all_to_all(right_sum, 'col', split_axis=0, concat_axis=1, tiled=True)]
    another operation x0 -> x2, local copies, waits for them, and re-layouts: none -> 5.94 us  [the longest x1 2.97 us: shards(): right_sum.reshape(n_col, share, cols * size)]
    all_to_all x2 -> x0, local copies, waits for them, and re-layouts: 3.1 us -> none  [shards(): lax.all_to_all(right_sum, 'col', split_axis=0, concat_axis=1, tiled=True)]
  transfers between devices with their start and end apart: 4 -> 1, of which waited for: 1 -> 0; matrix products, arithmetic and copies ran while one was open for 10% -> 7% of each run, Pallas kernels for 0% -> 0%
where the time goes in v2:
time: 203 us; the launch traced here: 202 us
  Pallas kernels  117 us (58%)
  local copies, waits for them, and re-layouts  41.8 us (21%)
  blocking collectives  31.4 us (15%)
  other arithmetic  5.56 us (3%)
  starting transfers between devices  4.87 us (2%)
    pallas_call x1, Pallas kernels, shards(): pl.pallas_call(functools.partial(pair_kernel, group, cols, seqs, levels),...  63.5 us
    pallas_call x1, Pallas kernels, shards(): pl.pallas_call(functools.partial(sum_kernel, n_row, n_col, ratio), in_spe...  53.2 us
    all_gather x1, blocking collectives, shards(): left_panel = lax.all_gather(first_factor, 'col', axis=0, tiled=True)  22.7 us
    all_gather x1, blocking collectives, shards(): right_rows = lax.all_gather(second_factor, 'row', axis=1, tiled=True)  8.65 us
    all_to_all x1, starting transfers between devices, shards(): lax.all_to_all(right_rows, 'col', split_axis=1, concat_axis=0, tiled=True)  4.87 us
    reshape x1, local copies, waits for them, and re-layouts, shards(): left_levels = left_panel.reshape(levels, DEPTH_STEP, steps, group, size)....  4.23 us
  transfers between devices with their start and end apart: 1, of which 0 were waited for; matrix products, arithmetic and copies ran while one was open for 7% of the time, Pallas kernels for 0%

profile of v2, /device:TPU:0, one launch (start us, length us, event | category | flops | bytes accessed | tf_op | source)
XLA Modules:
  0.0 202.2 jit_solution(13278679215754601313)
XLA Ops:
  0.6 0.0 copy-start
  0.7 1.6 convert_reduce_fusion
  2.3 1.9 fusion.2
  4.3 0.7 fusion.5
  5.0 0.4 convolution_convert_fusion
  5.5 0.0 copy-start.9
  5.5 0.0 copy-start.10
  5.5 0.3 copy.46
  5.8 0.5 reshape.91
  6.3 8.6 %all_gather.7 = bf16[32,8192]{1,0:T(8,128)(2,1)S(1)} all-gather(bf16[32,2048]{1,0:T(8,128)(2,1)S(1)} %reshape.91), channel_id=1, replica_groups=mesh['parts'=2,'row'=4,'col'=4] {'row'}, dimensions={1}, use_global_device_ids=true | all-gather | bytes 655360 | tf_op jit(solution)/shard_map/all_gather | solution.py:282
  15.0 0.8 copy.65
  15.8 4.9 %all-to-all-start = ((bf16[32,4,2048]{2,0,1:T(8,128)(2,1)}), bf16[32,4,2048]{2,0,1:T(8,128)(2,1)S(1)}, u32[]{:S(2)}, u32[]{:S(2)}) async-start(bf16[32,4,2048]{2,0,1:T(8,128)(2,1)} %bitcast.43), calls=%async_computation | async-start | bytes 1048576 | tf_op jit(solution)/shard_map/all_to_all | solution.py:283
  20.7 0.1 fusion.16
  20.8 0.2 fusion.9
  21.0 0.3 fusion.10
  21.2 0.1 broadcast_in_dim.10
  21.3 0.7 reshape.94.depth_ref
  22.0 0.3 copy.43
  22.3 0.5 reshape.88
  22.8 0.0 copy-start.2
  22.8 22.7 %all_gather.6 = bf16[128,2048]{1,0:T(8,128)(2,1)S(1)} all-gather(bf16[32,2048]{1,0:T(8,128)(2,1)S(1)} %reshape.88), channel_id=1, replica_groups=mesh['parts'=2,'row'=4,'col'=4] {'col'}, dimensions={0}, use_global_device_ids=true | all-gather | bytes 655360 | tf_op jit(solution)/shard_map/all_gather | solution.py:281
  45.6 1.0 copy.44
  46.6 1.6 reshape.98
  48.2 0.1 copy.49
  48.3 0.8 copy.50
  49.2 1.9 copy.64
  51.1 1.7 copy.51
  52.8 4.2 %reshape.99.left_t_ref = bf16[4,64,1024]{2,1,0:T(8,128)(2,1)} reshape(bf16[4,2,32,32,32]{4,3,2,1,0:T(8,128)(2,1)} %copy.51) | data formatting | bytes 1048576 | tf_op jit(solution)/shard_map/reshape | solution.py:309
  57.1 0.0 all-to-all-done
  57.1 1.6 reshape.92
  58.7 2.6 %copy.48 = bf16[128,32,64]{0,2,1:T(8,128)(2,1)S(1)} copy(bf16[128,32,64]{1,2,0:T(8,128)(2,1)S(1)} %bitcast.44) | data formatting | bytes 1048576 | tf_op jit(solution)/shard_map/transpose | solution.py:311
  61.3 2.0 broadcast_in_dim.8
  63.3 0.3 copy.63
  63.6 3.0 %copy.52.right_ref = bf16[256,4096]{1,0:T(8,128)(2,1)} copy(bf16[256,4096]{0,1:T(8,128)(2,1)S(1)} %bitcast.49) | data formatting | bytes 4194304 | tf_op jit(solution)/shard_map/reshape | solution.py:314
  66.6 0.9 broadcast_in_dim.11
  67.5 63.5 %shard_map.129 = (bf16[4096,128]{1,0:T(8,128)(2,1)}, bf16[32,32,256]{2,1,0:T(8,128)(2,1)}, f32[128,4096]{1,0:T(8,128)}, f32[1024,128]{1,0:T(8,128)}) custom-call(bf16[32,32,256]{2,1,0:T(8,128)(2,1)} %bitcast.58, bf16[256,4096]{1,0:T(8,128)(2,1)} %copy.52.right_ref, f32[32,1,128]{2,1,0:T(1,128)} %reshape.94.depth_ref, bf16[4096,128]{1,0:T(8,128)(2,1)} %bitcast.60, ...), custom_call_target="tpu_custom_call" | custom-call | tf_op jit(solution)/shard_map/pallas_call | solution.py:320
  131.0 1.2 reshape.102
  132.2 2.0 copy.53
  134.2 3.0 %reshape_reshape.6.left_ref = bf16[4,32,2048]{2,1,0:T(8,128)(2,1)} reshape(bf16[128,32,2,32]{3,2,1,0:T(2,128)(2,1)S(1)} %bitcast.45) | data formatting | bytes 1048576 | tf_op jit(solution)/shard_map/reshape;reshape | solution.py:409
  137.1 1.9 copy.54
  139.0 0.2 reduce_sum.29
  139.2 3.2 %copy.55 = bf16[128,64,32]{2,1,0:T(8,128)(2,1)S(1)} copy(bf16[128,64,32]{0,1,2:T(8,128)(2,1)S(1)} %bitcast.56) | data formatting | bytes 1048576 | tf_op jit(solution)/shard_map/convert_element_type | solution.py:372
  142.5 3.0 %reshape_reshape.7.right_ref = bf16[4,32,2048]{2,1,0:T(8,128)(2,1)} reshape(bf16[128,64,32]{2,1,0:T(8,128)(2,1)S(1)} %copy.55) | data formatting | bytes 1048576 | tf_op jit(solution)/shard_map/reshape;reshape | solution.py:410
  145.4 53.2 %shard_map.130 = (bf16[32,2048]{1,0:T(8,128)(2,1)}, bf16[32,2048]{1,0:T(8,128)(2,1)}, f32[1024,128]{1,0:T(8,128)}) custom-call(bf16[4,32,2048]{2,1,0:T(8,128)(2,1)} %reshape_reshape.6.left_ref, bf16[4,32,2048]{2,1,0:T(8,128)(2,1)} %reshape_reshape.7.right_ref, f32[1024,128]{1,0:T(8,128)} %get-tuple-element.14.weight_ref), custom_call_target="tpu_custom_call" | custom-call | tf_op jit(solution)/shard_map/pallas_call | solution.py:383
  198.7 1.1 broadcast_multiply_fusion
  199.8 1.1 copy.56
  200.9 0.7 copy.68
  201.6 0.7 copy.69
  (21 shorter events, 0.1 us)
Async XLA Ops:
  0.6 3.6 %copy-start = (bf16[32,64,256]{2,1,0:T(8,128)(2,1)S(1)}, bf16[32,64,256]{2,1,0:T(8,128)(2,1)}, u32[]{:S(2)}) copy-start(bf16[32,64,256]{2,1,0:T(8,128)(2,1)} %param.10) | copy-start | bytes 3145732
  0.6 3.6 %copy-start.7 = (f32[256]{0:T(256)S(1)}, f32[256]{0:T(256)}, u32[]{:S(2)}) copy-start(f32[256]{0:T(256)} %param.12) | copy-start | bytes 3076
  0.7 3.6 %copy-start.8 = (f32[256]{0:T(256)S(1)}, f32[256]{0:T(256)}, u32[]{:S(2)}) copy-start(f32[256]{0:T(256)} %param.11) | copy-start | bytes 3076
  0.7 4.3 %copy-start.5 = (bf16[256,32]{0,1:T(8,128)(2,1)S(1)}, bf16[256,32]{0,1:T(8,128)(2,1)}, u32[]{:S(2)}) copy-start(bf16[256,32]{0,1:T(8,128)(2,1)} %param.14) | copy-start | bytes 49156
  0.7 4.3 %copy-start.6 = (bf16[256,32]{0,1:T(8,128)(2,1)S(1)}, bf16[256,32]{0,1:T(8,128)(2,1)}, u32[]{:S(2)}) copy-start(bf16[256,32]{0,1:T(8,128)(2,1)} %param.13) | copy-start | bytes 49156
  5.5 15.2 %copy-start.9 = (s32[256]{0:T(256)S(1)}, s32[256]{0:T(256)}, u32[]{:S(2)}) copy-start(s32[256]{0:T(256)} %param.17) | copy-start | bytes 3076
  5.5 15.3 %copy-start.10 = (s32[8,8]{1,0:T(8,128)S(1)}, s32[8,8]{1,0:T(8,128)}, u32[]{:S(2)}) copy-start(s32[8,8]{1,0:T(8,128)} %param.18) | copy-start | bytes 772
  15.8 41.3 %all-to-all-start = ((bf16[32,4,2048]{2,0,1:T(8,128)(2,1)}), bf16[32,4,2048]{2,0,1:T(8,128)(2,1)S(1)}, u32[]{:S(2)}, u32[]{:S(2)}) async-start(bf16[32,4,2048]{2,0,1:T(8,128)(2,1)} %bitcast.43), calls=%async_computation | async-start | bytes 1048576 | tf_op jit(solution)/shard_map/all_to_all | solution.py:283
  22.8 25.4 %copy-start.2 = (bf16[1024,128]{1,0:T(8,128)(2,1)S(1)}, bf16[1024,128]{1,0:T(8,128)(2,1)}, u32[]{:S(2)}) copy-start(bf16[1024,128]{1,0:T(8,128)(2,1)} %param.15) | copy-start | bytes 786436
  48.3 4.5 %copy-start.1 = (bf16[32,32,128]{2,1,0:T(8,128)(2,1)}, bf16[32,32,128]{2,1,0:T(8,128)(2,1)S(1)}, u32[]{:S(2)}) copy-start(bf16[32,32,128]{2,1,0:T(8,128)(2,1)S(1)} %copy.49) | copy-start | bytes 786436
  198.7 2.2 %copy-start.4 = (bf16[32,2048]{1,0:T(8,128)(2,1)S(1)}, bf16[32,2048]{1,0:T(8,128)(2,1)}, u32[]{:S(2)}) copy-start(bf16[32,2048]{1,0:T(8,128)(2,1)} %get-tuple-element.27) | copy-start | bytes 393220
  198.7 2.9 %copy-start.3 = (bf16[32,2048]{1,0:T(8,128)(2,1)S(1)}, bf16[32,2048]{1,0:T(8,128)(2,1)}, u32[]{:S(2)}) copy-start(bf16[32,2048]{1,0:T(8,128)(2,1)} %get-tuple-element.28) | copy-start | bytes 393220
